TPU v7x, 32 devices: a whole 2x2x4 slice. The times are simulated.
32 devices in a mesh: dp: 8 (over y, x, core), tensor: 4 (over z).
Axes of the slice: x: 2, y: 2, z: 4, core: 2. Of those that a mesh axis runs over, the one named last changes fastest.
Arguments:
- hidden_in: bfloat16 [16384, 1024], P('dp'), may hold values from -6 to 6
- lengths: int32 [8], P('dp'), may hold values from 512 to 2048, as said below
- query_weight: bfloat16 [1024, 1024], P(None, 'tensor'), may hold values from -0.1875 to 0.1875
- query_bias: bfloat16 [1024], P('tensor'), may hold values from -1 to 1
- key_weight: bfloat16 [1024, 1024], P(None, 'tensor'), may hold values from -0.1875 to 0.1875
- value_weight: bfloat16 [1024, 1024], P(None, 'tensor'), may hold values from -0.1875 to 0.1875
- value_bias: bfloat16 [1024], P('tensor'), may hold values from -1 to 1
- output_weight: bfloat16 [1024, 1024], P(None, 'tensor'), may hold values from -2 to 2
- output_bias: bfloat16 [1024], replicated, may hold values from -1 to 1
- first_gain: bfloat16 [1024], replicated, may hold values from 0.5 to 1.5
- first_shift: bfloat16 [1024], replicated, may hold values from -1 to 1
- inner_weight: bfloat16 [1024, 4096], P(None, 'tensor'), may hold values from -0.1875 to 0.1875
- inner_bias: bfloat16 [4096], P('tensor'), may hold values from -1 to 1
- outer_weight: bfloat16 [1024, 4096], P(None, 'tensor'), may hold values from -0.125 to 0.125
- outer_bias: bfloat16 [1024], replicated, may hold values from -1 to 1
- second_gain: bfloat16 [1024], replicated, may hold values from 0.5 to 1.5
- second_shift: bfloat16 [1024], replicated, may hold values from -1 to 1
- cotangent: bfloat16 [16384, 1024], P('dp'), may hold values from -6 to 6
- teacher: bfloat16 [16384, 1024], P('dp'), may hold values from -6 to 6
Outputs:
- layer_output: bfloat16 [16384, 1024], P(('dp', 'tensor'))
- distill_loss: float32 [], replicated
- input_grad: float32 [16384, 1024], P(('dp', 'tensor'))
- query_weight_grad: float32 [1024, 1024], P('dp', 'tensor')
- query_bias_grad: float32 [1024], replicated
- key_weight_grad: float32 [1024, 1024], P('dp', 'tensor')
- value_weight_grad: float32 [1024, 1024], P('dp', 'tensor')
- value_bias_grad: float32 [1024], replicated
- output_weight_grad: float32 [1024, 1024], P('dp', 'tensor')
- output_bias_grad: float32 [1024], replicated
- first_gain_grad: float32 [1024], replicated
- first_shift_grad: float32 [1024], replicated
- inner_weight_grad: float32 [1024, 4096], P('dp', 'tensor')
- inner_bias_grad: float32 [4096], replicated
- outer_weight_grad: float32 [1024, 4096], P('dp', 'tensor')
- outer_bias_grad: float32 [1024], replicated
- second_gain_grad: float32 [1024], replicated
- second_shift_grad: float32 [1024], replicated
Inputs may be any that keep to these rules, and one draw needn't show every extreme that they name: `lengths`: one sequence's valid tokens; slots after them are padding; some sequence fills all 2048 slots.
All inputs are finite; a program needn't handle non-finite values.
Results may differ from a plain program's by a relative error of at most 0.018.
Values may be sent and summed in bfloat16 or wider, within the bound.
No kernel may reach another device: no remote copies, remote signals or barrier semaphores. Data moves between devices by JAX's collectives and lax.ppermute only.
A program may use at most 256 MiB of HBM per device.

v0:
```python
import math
import jax
import jax.numpy as jnp
from jax import lax
from jax.sharding import PartitionSpec as P

HD = 64
epsilon = 1e-05


def matmul(former, latter):
    return jnp.dot(former, latter, preferred_element_type=jnp.float32)


def times_rows(former, latter):
    return lax.dot_general(
        former, latter, (((1,), (1,)), ((), ())), preferred_element_type=jnp.float32
    )


def over_rows(former, latter):
    return lax.dot_general(
        former, latter, (((0,), (0,)), ((), ())), preferred_element_type=jnp.float32
    )


def layer_norm(hidden, norm_gain, norm_shift):
    centered = hidden - jnp.mean(hidden, axis=-1, keepdims=True)
    inverse = lax.rsqrt(jnp.mean(centered * centered, axis=-1, keepdims=True) + epsilon)
    normal = centered * inverse
    return (normal * norm_gain + norm_shift, normal, inverse)


def norm_back(upstream, normal, inverse, norm_gain):
    scaled = upstream * norm_gain
    return inverse * (
        scaled
        - jnp.mean(scaled, axis=-1, keepdims=True)
        - normal * jnp.mean(scaled * normal, axis=-1, keepdims=True)
    )


def gelu_exact(values):
    return 0.5 * values * (1.0 + jax.scipy.special.erf(values * 0.7071067811865476))


def gelu_slope(values):
    return (
        0.5 * (1.0 + jax.scipy.special.erf(values * 0.7071067811865476))
        + values * jnp.exp(-0.5 * values * values) * 0.3989422804014327
    )


def split_blocks(queries, keys_all, values_all):
    seq_len, local_width = queries.shape
    heads_here = local_width // HD
    block_rows = min(512, seq_len)
    block_count = seq_len // block_rows
    keys_split = keys_all.reshape(seq_len, heads_here, HD)
    values_split = values_all.reshape(seq_len, heads_here, HD)
    query_blocks = queries.reshape(block_count, block_rows, heads_here, HD)
    return (keys_split, values_split, query_blocks, block_count, block_rows, heads_here)


def block_scores(query_block, keys_split, key_valid, score_scale):
    scores = (
        jnp.einsum("qhd,khd->hqk", query_block, keys_split, preferred_element_type=jnp.float32)
        * score_scale
    )
    return jnp.where(key_valid[None, None, :], scores, -1e30)


def attend_forward(queries, keys_all, values_all, key_valid, score_scale):
    keys_split, values_split, query_blocks, block_count, block_rows, heads_here = split_blocks(
        queries, keys_all, values_all
    )

    def one_block(query_block):
        scores = block_scores(query_block, keys_split, key_valid, score_scale)
        row_peak = jnp.max(scores, axis=-1, keepdims=True)
        exponent = jnp.exp(scores - row_peak)
        row_total = jnp.sum(exponent, axis=-1, keepdims=True)
        probs = (exponent / row_total).astype(jnp.bfloat16)
        context = jnp.einsum(
            "hqk,khd->qhd", probs, values_split, preferred_element_type=jnp.float32
        )
        return (context, (row_peak + jnp.log(row_total))[..., 0])

    context, logsum = lax.map(one_block, query_blocks)
    return (context.reshape(queries.shape), logsum)


def attend_backward(queries, keys_all, values_all, key_valid, score_scale, logsum, context_grad):
    keys_split, values_split, query_blocks, block_count, block_rows, heads_here = split_blocks(
        queries, keys_all, values_all
    )
    grad_blocks = context_grad.reshape(block_count, block_rows, heads_here, HD)

    def one_block(carry, inputs):
        key_sum, value_sum = carry
        query_block, grad_block, logsum_block = inputs
        scores = block_scores(query_block, keys_split, key_valid, score_scale)
        probs = jnp.exp(scores - logsum_block[..., None])
        prob_grad = jnp.einsum(
            "qhd,khd->hqk", grad_block, values_split, preferred_element_type=jnp.float32
        )
        centre = jnp.sum(probs * prob_grad, axis=-1, keepdims=True)
        score_grad = (probs * (prob_grad - centre)).astype(jnp.bfloat16)
        query_grad = (
            jnp.einsum("hqk,khd->qhd", score_grad, keys_split, preferred_element_type=jnp.float32)
            * score_scale
        )
        key_sum = (
            key_sum
            + jnp.einsum(
                "hqk,qhd->khd", score_grad, query_block, preferred_element_type=jnp.float32
            )
            * score_scale
        )
        value_sum = value_sum + jnp.einsum(
            "hqk,qhd->khd",
            probs.astype(jnp.bfloat16),
            grad_block,
            preferred_element_type=jnp.float32,
        )
        return ((key_sum, value_sum), query_grad)

    zero_block = jnp.zeros(keys_split.shape, jnp.float32)
    (key_sum, value_sum), query_grads = lax.scan(
        one_block, (zero_block, zero_block), (query_blocks, grad_blocks, logsum)
    )
    return (
        query_grads.reshape(queries.shape),
        key_sum.reshape(queries.shape),
        value_sum.reshape(queries.shape),
    )


def shards(
    hidden_in,
    lengths,
    query_weight,
    query_bias,
    key_weight,
    value_weight,
    value_bias,
    output_weight,
    output_bias,
    first_gain,
    first_shift,
    inner_weight,
    inner_bias,
    outer_weight,
    outer_bias,
    second_gain,
    second_shift,
    cotangent,
    teacher,
):
    seq_len, model_width = hidden_in.shape
    tensor_size = lax.axis_size("tensor")
    tensor_index = lax.axis_index("tensor")
    share_rows = seq_len // tensor_size
    row_start = tensor_index * share_rows
    score_scale = 1.0 / math.sqrt(HD)
    positions = jnp.arange(seq_len, dtype=jnp.int32)
    row_valid = positions < lengths[0]
    token_total = lax.psum(jnp.sum(lengths), "dp").astype(jnp.float32)
    grad_scale = seq_len * lax.axis_size("dp") / (2.0 * token_total)
    hidden_float = hidden_in.astype(jnp.float32)
    queries = (matmul(hidden_in, query_weight) + query_bias).astype(jnp.bfloat16)
    keys_all = matmul(hidden_in, key_weight).astype(jnp.bfloat16)
    values_all = (matmul(hidden_in, value_weight) + value_bias).astype(jnp.bfloat16)
    context, logsum = attend_forward(queries, keys_all, values_all, row_valid, score_scale)
    context_low = context.astype(jnp.bfloat16)
    attention_part = times_rows(context_low, output_weight)

    def take_own(array_in):
        return lax.dynamic_slice_in_dim(array_in, row_start, share_rows, 0)

    attention_whole = lax.psum(attention_part, "tensor")
    normed, normal_one, inverse_one = layer_norm(
        hidden_float + (attention_whole + output_bias), first_gain, first_shift
    )
    normed_low = normed.astype(jnp.bfloat16)
    inner = matmul(normed_low, inner_weight) + inner_bias
    activated = gelu_exact(inner).astype(jnp.bfloat16)
    outer_part = times_rows(activated, outer_weight)
    outer_rows = lax.psum(outer_part, "tensor")
    final, normal_two, inverse_two = layer_norm(
        normed + (outer_rows + outer_bias), second_gain, second_shift
    )
    row_mask = row_valid[:, None]
    difference = final - teacher.astype(jnp.float32)
    loss_part = jnp.sum(take_own(jnp.where(row_mask, difference * difference, 0.0)))
    final_grad = jnp.where(row_mask, cotangent.astype(jnp.float32) + grad_scale * difference, 0.0)
    second_grad = norm_back(final_grad, normal_two, inverse_two, second_gain)
    branch_low = second_grad.astype(jnp.bfloat16)
    activated_grad = matmul(branch_low, outer_weight)
    outer_weight_grad = over_rows(branch_low, activated)
    inner_low = (activated_grad * gelu_slope(inner)).astype(jnp.bfloat16)
    inner_bias_grad = jnp.sum(inner_low.astype(jnp.float32), axis=0)
    inner_weight_grad = over_rows(normed_low, inner_low)
    normed_part = times_rows(inner_low, inner_weight)
    normed_back = lax.psum(normed_part, "tensor")
    normed_grad = second_grad + normed_back
    first_grad = norm_back(normed_grad, normal_one, inverse_one, first_gain)
    attention_low = first_grad.astype(jnp.bfloat16)
    output_weight_grad = over_rows(attention_low, context_low)
    context_grad = matmul(attention_low, output_weight).astype(jnp.bfloat16)
    query_grad, key_grad, value_grad = attend_backward(
        queries, keys_all, values_all, row_valid, score_scale, logsum, context_grad
    )
    query_low = query_grad.astype(jnp.bfloat16)
    key_low = key_grad.astype(jnp.bfloat16)
    value_low = value_grad.astype(jnp.bfloat16)
    input_part = (
        times_rows(query_low, query_weight)
        + times_rows(key_low, key_weight)
        + times_rows(value_low, value_weight)
    )
    input_back = lax.psum(input_part.astype(jnp.bfloat16), "tensor").astype(jnp.float32)
    input_rows = take_own(input_back) + take_own(first_grad)
    weight_grads = (
        lax.psum_scatter(
            over_rows(hidden_in, query_low).astype(jnp.bfloat16),
            "dp",
            scatter_dimension=0,
            tiled=True,
        ).astype(jnp.float32),
        lax.psum_scatter(
            over_rows(hidden_in, key_low).astype(jnp.bfloat16),
            "dp",
            scatter_dimension=0,
            tiled=True,
        ).astype(jnp.float32),
        lax.psum_scatter(
            over_rows(hidden_in, value_low).astype(jnp.bfloat16),
            "dp",
            scatter_dimension=0,
            tiled=True,
        ).astype(jnp.float32),
        lax.psum_scatter(
            output_weight_grad.astype(jnp.bfloat16), "dp", scatter_dimension=0, tiled=True
        ).astype(jnp.float32),
        lax.psum_scatter(
            inner_weight_grad.astype(jnp.bfloat16), "dp", scatter_dimension=0, tiled=True
        ).astype(jnp.float32),
        lax.psum_scatter(
            outer_weight_grad.astype(jnp.bfloat16), "dp", scatter_dimension=0, tiled=True
        ).astype(jnp.float32),
    )

    def placed(vector_in):
        full_zeros = jnp.zeros((vector_in.shape[0] * tensor_size,), jnp.float32)
        return lax.dynamic_update_slice_in_dim(
            full_zeros, vector_in, tensor_index * vector_in.shape[0], 0
        )

    vector_grads = lax.psum(
        (
            placed(jnp.sum(query_low.astype(jnp.float32), axis=0)),
            placed(jnp.sum(value_low.astype(jnp.float32), axis=0)),
            jnp.sum(take_own(attention_low).astype(jnp.float32), axis=0),
            jnp.sum(take_own(normed_grad * normal_one), axis=0),
            jnp.sum(take_own(normed_grad), axis=0),
            placed(inner_bias_grad),
            jnp.sum(take_own(branch_low).astype(jnp.float32), axis=0),
            jnp.sum(take_own(final_grad * normal_two), axis=0),
            jnp.sum(take_own(final_grad), axis=0),
            loss_part,
        ),
        ("dp", "tensor"),
    )
    (
        query_bias_grad,
        value_bias_grad,
        output_bias_grad,
        first_gain_grad,
        first_shift_grad,
        inner_bias_full,
        outer_bias_grad,
        second_gain_grad,
        second_shift_grad,
        loss_total,
    ) = vector_grads
    (
        query_weight_grad,
        key_weight_grad,
        value_weight_grad,
        output_weight_sum,
        inner_weight_sum,
        outer_weight_sum,
    ) = weight_grads
    distill_loss = loss_total / token_total
    return (
        take_own(final).astype(jnp.bfloat16),
        distill_loss,
        input_rows,
        query_weight_grad,
        query_bias_grad,
        key_weight_grad,
        value_weight_grad,
        value_bias_grad,
        output_weight_sum,
        output_bias_grad,
        first_gain_grad,
        first_shift_grad,
        inner_weight_sum,
        inner_bias_full,
        outer_weight_sum,
        outer_bias_grad,
        second_gain_grad,
        second_shift_grad,
    )


def solution(mesh):
    in_specs = (
        P("dp", None),
        P("dp"),
        P(None, "tensor"),
        P("tensor"),
        P(None, "tensor"),
        P(None, "tensor"),
        P("tensor"),
        P(None, "tensor"),
        P(),
        P(),
        P(),
        P(None, "tensor"),
        P("tensor"),
        P(None, "tensor"),
        P(),
        P(),
        P(),
        P("dp", None),
        P("dp", None),
    )
    out_specs = (
        P(("dp", "tensor"), None),
        P(),
        P(("dp", "tensor"), None),
        P("dp", "tensor"),
        P(),
        P("dp", "tensor"),
        P("dp", "tensor"),
        P(),
        P("dp", "tensor"),
        P(),
        P(),
        P(),
        P("dp", "tensor"),
        P(),
        P("dp", "tensor"),
        P(),
        P(),
        P(),
    )
    return jax.shard_map(shards, mesh=mesh, in_specs=in_specs, out_specs=out_specs, check_vma=False)
```

profile of v0, /device:TPU:0, one launch (start us, length us, event | category | flops | bytes accessed | tf_op | source)
XLA Modules:
  0.0 1564.1 jit_solution(17279428161375169190)
XLA Ops:
  25.2 55.2 %while.28 = (s32[]{:T(128)}, bf16[4,512,4,64]{1,3,2,0:T(8,128)(2,1)}, f32[4,4,512]{2,1,0:T(4,128)S(1)}, bf16[4,512,4,64]{1,3,2,0:T(8,128)(2,1)}, bf16[2048,4,64]...) while((s32[]{:T(128)}, bf16[4,512,4,64]{1,3,2,0:T(8,128)(2,1)}, ...), condition=%wide.region_3.4_spmd.clone, body=%wide.region_0.3_spmd.clone.sunk | while | flops 1124073472 | bytes 65872064 | solution.py:89
  33.2 4.9 fusion.138
  47.0 4.9 fusion.138
  60.8 4.9 fusion.138
  74.6 4.9 fusion.138
  83.8 5.6 fusion.70
  89.8 293.4 %all-reduce.6.cloned.1.call-done = f32[2048,1024]{1,0:T(8,128)} async-done(((f32[2048,1024]{1,0:T(8,128)}), f32[2048,1024]{1,0:T(8,128)}) %all-reduce.6.cloned.1.call-update) | async-done | bytes 8388624 | tf_op jit(solution)/shard_map/psum | solution.py:181
  383.2 5.9 fusion.54
  394.8 7.4 multiply_convert_fusion.1
  404.1 6.9 fusion.71
  411.0 8.8 psum.108
  421.3 279.7 %all-reduce.8.cloned.1.call-done = f32[2048,1024]{1,0:T(8,128)} async-done(((f32[2048,1024]{1,0:T(8,128)}), f32[2048,1024]{1,0:T(8,128)}) %all-reduce.8.cloned.1.call-update) | async-done | bytes 8388624 | tf_op jit(solution)/shard_map/psum | solution.py:189
  701.0 6.7 fusion.69
  708.8 10.9 multiply_reduce_fusion.6
  725.8 11.3 convert_reduce_fusion
  739.1 6.9 fusion.72
  746.5 9.4 convolution_convert_fusion.2
  756.0 10.5 convolution_convert_fusion.3
  766.7 269.2 %all-reduce.10.cloned.1.call-done = f32[2048,1024]{1,0:T(8,128)} async-done(((f32[2048,1024]{1,0:T(8,128)}), f32[2048,1024]{1,0:T(8,128)}) %all-reduce.10.cloned.1.call-update) | async-done | bytes 8388624 | tf_op jit(solution)/shard_map/psum | solution.py:205
  1036.0 16.3 %multiply_reduce_fusion.5 = (f32[2048]{0:T(1024)S(1)}, f32[2048]{0:T(1024)S(1)}, f32[2048,1024]{1,0:T(8,128)}) fusion(f32[1024]{0:T(1024)S(1)} %convert_element_type.183, f32[2048,1024]{1,0:T(8,128)} %copy-done.5, f32[2048,1024]{1,0:T(8,128)} %all-reduce.10.cloned.1.call-done, f32[2048,1024]{1,0:T(8,128)} %copy-done.7, f32[2048]{0:T(1024)S(1)} %get-tuple-element.345, ...), kind=kLoop, calls=%fused_computation.76 | loop fusion | flops 20967424 | bytes 41992192 | tf_op jit(solution)/shard_map/reduce_sum | solution.py:38
  1052.4 9.8 fusion.67
  1066.3 4.4 reshape.147
  1076.0 166.5 %while.29 = (s32[]{:T(128)}, f32[2048,4,64]{0,2,1:T(8,128)S(1)}, f32[2048,4,64]{0,2,1:T(8,128)}, bf16[4,512,4,64]{1,3,2,0:T(8,128)(2,1)}, bf16[4,512,4,64]{1,3,2...) while((s32[]{:T(128)}, f32[2048,4,64]{0,2,1:T(8,128)S(1)}, ...), condition=%wide.region_20.21_spmd.clone, body=%wide.region_18.20_spmd.clone.sunk | while | flops 2750021632 | bytes 180945136 | solution.py:129
  1080.9 5.8 fusion.150
  1086.7 10.1 multiply_reduce_fusion.8
  1096.8 11.0 multiply_convert_fusion.3
  1107.8 7.2 fusion.151
  1122.6 6.2 fusion.150
  1128.8 9.9 multiply_reduce_fusion.8
  1138.7 10.6 multiply_convert_fusion.3
  1149.3 7.1 fusion.151
  1164.0 6.2 fusion.150
  1170.2 9.9 multiply_reduce_fusion.8
  1180.1 10.6 multiply_convert_fusion.3
  1190.7 7.1 fusion.151
  1205.5 6.2 fusion.150
  1211.7 9.9 multiply_reduce_fusion.8
  1221.6 10.6 multiply_convert_fusion.3
  1232.2 7.1 fusion.151
  1262.3 5.7 fusion.74
  1268.0 4.4 convolution_convert_fusion.4
  1272.5 4.5 fusion.73
  1277.1 9.1 add_convert_fusion
  1291.3 4.6 dynamic-slice_reduce_fusion
  1304.3 40.3 %all-reduce = (f32[]{:T(128)}, f32[1024]{0:T(1024)}, f32[1024]{0:T(1024)}, f32[1024]{0:T(1024)}, f32[1024]{0:T(1024)}, /*index=5*/f32[1024]{0:T(1024)}, f32[4096...) all-reduce(f32[]{:T(128)} %get-tuple-element.344, ...), channel_id=1, replica_groups=mesh['dp'=8,'tensor'=4] {'dp','tensor'}, use_global_device_ids=true, to_apply=%region_11.12 | all-reduce | flops 12289 | bytes 98312 | tf_op jit(solution)/shard_map/psum | solution.py:260
  1348.7 8.8 reduce-scatter.23.cloned.1.call-done
  1359.3 35.5 %reduce-scatter.13.cloned.1.call-done = bf16[128,256]{1,0:T(8,128)(2,1)} async-done(((bf16[1024,256]{1,0:T(8,128)(2,1)}), bf16[128,256]{1,0:T(8,128)(2,1)}) %reduce-scatter.13.cloned.1.call-update) | async-done | bytes 65552 | tf_op jit(solution)/shard_map/reduce_scatter | solution.py:243
  1396.3 155.7 %all-reduce.12.cloned.1.call-done = bf16[2048,1024]{1,0:T(8,128)(2,1)} async-done(((bf16[2048,1024]{1,0:T(8,128)(2,1)}), bf16[2048,1024]{1,0:T(8,128)(2,1)}) %all-reduce.12.cloned.1.call-update) | async-done | bytes 4194320 | tf_op jit(solution)/shard_map/psum | solution.py:222
  (241 shorter events, 157.9 us)
Async XLA Ops:
  7.2 387.5 %copy-start = (bf16[1024,1024]{1,0:T(8,128)(2,1)S(1)}, bf16[1024,1024]{1,0:T(8,128)(2,1)}, u32[]{:S(2)}) copy-start(bf16[1024,1024]{1,0:T(8,128)(2,1)} %param.34) | copy-start | bytes 6291460
  7.2 376.0 %all-reduce.6.cloned.1.call-start = ((), (), s32[]{:S(2)}) async-start(), calls=%async_computation.6 | async-start | bytes 16777216 | tf_op jit(solution)/shard_map/psum | solution.py:181
  18.1 3.8 copy-start.25
  29.4 3.8 copy-start.11
  29.4 3.8 copy-start.21
  43.2 3.8 copy-start.11
  43.2 3.8 copy-start.21
  57.0 3.8 copy-start.11
  57.0 3.8 copy-start.21
  70.8 3.8 copy-start.11
  70.8 3.8 copy-start.21
  83.8 5.9 copy-start.29
  83.8 5.9 copy-start.30
  83.8 6.0 copy-start.31
  83.8 6.0 copy-start.32
  89.5 611.5 %all-reduce.8.cloned.1.call-start = ((), (), s32[]{:S(2)}) async-start(), calls=%async_computation.7 | async-start | bytes 16777216 | tf_op jit(solution)/shard_map/psum | solution.py:189
  383.2 7.0 copy-start.8
  383.2 8.2 copy-start.10
  394.7 7.4 copy-start.5
  394.8 9.3 copy-start.36
  411.0 10.2 copy-start.33
  411.0 10.2 copy-start.34
  411.0 10.2 copy-start.35
  411.0 625.0 %all-reduce.10.cloned.1.call-start = ((), (), s32[]{:S(2)}) async-start(), calls=%async_computation.8 | async-start | bytes 16777216 | tf_op jit(solution)/shard_map/psum | solution.py:205
  421.3 287.5 %copy-start.27 = (pred[2048]{0:T(1024)(128)(4,1)}, pred[2048]{0:T(1024)(128)(4,1)S(1)}, u32[]{:S(2)}) copy-start(pred[2048]{0:T(1024)(128)(4,1)S(1)} %iota_compare_fusion.2) | copy-start | bytes 6148
  719.7 6.1 copy-start.7
  719.7 6.1 copy-start.37
  725.8 11.3 copy-start.13
  746.0 549.9 %reduce-scatter.17.cloned.1.call-start = ((), (), s32[]{:S(2)}) async-start(), calls=%async_computation.12 | async-start | bytes 2359296 | tf_op jit(solution)/shard_map/reduce_scatter | solution.py:249
  756.0 541.7 %reduce-scatter.15.cloned.1.call-start = ((), (), s32[]{:S(2)}) async-start(), calls=%async_computation.11 | async-start | bytes 2359296 | tf_op jit(solution)/shard_map/reduce_scatter | solution.py:246
  766.5 578.7 %reduce-scatter.19.cloned.1.call-start = ((), (), s32[]{:S(2)}) async-start(), calls=%async_computation.13 | async-start | bytes 589824
  1052.3 11.8 copy-start.23
  1107.8 7.2 copy-start.2
  1149.3 7.1 copy-start.2
  1190.7 7.2 copy-start.2
  1232.2 7.2 copy-start.2
  1250.3 96.8 %reduce-scatter.21.cloned.1.call-start = ((), (), s32[]{:S(2)}) async-start(), calls=%async_computation.14 | async-start | bytes 589824
  1256.8 100.8 %reduce-scatter.23.cloned.1.call-start = ((), (), s32[]{:S(2)}) async-start(), calls=%async_computation.15 | async-start | bytes 589824
  1261.2 6.8 copy-start.16
  1262.3 10.2 copy-start.18
  1267.9 4.5 copy-start.24
  1267.9 126.8 %reduce-scatter.13.cloned.1.call-start = ((), (), s32[]{:S(2)}) async-start(), calls=%async_computation.10 | async-start | bytes 589824 | tf_op jit(solution)/shard_map/reduce_scatter | solution.py:243
  1272.5 4.6 copy-start.20
  1272.5 4.6 copy-start.26
  1277.0 10.1 copy-start.28
  1277.0 275.0 %all-reduce.12.cloned.1.call-start = ((), (), s32[]{:S(2)}) async-start(), calls=%async_computation.9 | async-start | bytes 8388608 | tf_op jit(solution)/shard_map/psum | solution.py:222
  1286.2 13.3 copy-start.12
  1291.3 264.3 %copy-start.1 = (bf16[1024,1024]{1,0:T(8,128)(2,1)S(1)}, bf16[1024,1024]{1,0:T(8,128)(2,1)}, u32[]{:S(2)}) copy-start(bf16[1024,1024]{1,0:T(8,128)(2,1)} %param.34) | copy-start | bytes 6291460
  (20 other events, 35.5 us)
Sparse Core Ops, SparseCore 0:
  89.6 293.5 all-reduce.5
  411.1 289.7 all-reduce.7
  746.1 289.8 all-reduce.9
  1039.1 40.0 reduce-scatter.16
  1082.4 41.1 reduce-scatter.14
  1250.4 32.5 reduce-scatter.18
  1286.1 34.2 reduce-scatter.20
  1323.4 34.0 reduce-scatter.22
  1360.6 34.0 reduce-scatter.12
  1397.0 154.9 all-reduce.11
where the time goes:
time: 1570 us; the launch traced here: 1560 us
  waiting for transfers between devices  1040 us (66%)
  matrix products  256 us (16%)
  other arithmetic  142 us (9%)
  local copies, waits for them, and re-layouts  53.8 us (3%)
  blocking collectives  49.1 us (3%)
  between operations  18.3 us (1%)
    psum x1, waiting for transfers between devices, shards(): attention_whole = lax.psum(attention_part, 'tensor')  293 us
    psum x1, waiting for transfers between devices, shards(): outer_rows = lax.psum(outer_part, 'tensor')  280 us
    psum x1, waiting for transfers between devices, shards(): normed_back = lax.psum(normed_part, 'tensor')  269 us
    psum x1, waiting for transfers between devices, shards(): lax.psum(input_part.astype(jnp.bfloat16), 'tensor').astype(jnp.float32)  156 us
    convert_element_type x4, other arithmetic, one_block(): score_grad = (probs * (prob_grad - centre)).astype(jnp.bfloat16)  42.8 us
    psum x1, blocking collectives, shards(): lax.psum((placed(jnp.sum(query_low.astype(jnp.float32), axis=0)), placed(...  40.3 us
    dot_general x4, matrix products, one_block(): jnp.einsum('qhd,khd->hqk', grad_block, values_split, preferred_element_ty...  39.8 us
    dot_general x6, matrix products, times_rows(): lax.dot_general(former, latter, (((1,), (1,)), ((), ())), preferred_eleme...  38.7 us
  transfers between devices with their start and end apart: 10, of which 6 were waited for; matrix products, arithmetic and copies ran while one was open for 18% of the time, Pallas kernels for 0%

commit v1 on v0

--- a/solution.py
+++ b/solution.py
@@ -186,7 +186,11 @@
     inner = matmul(normed_low, inner_weight) + inner_bias
     activated = gelu_exact(inner).astype(jnp.bfloat16)
     outer_part = times_rows(activated, outer_weight)
-    outer_rows = lax.psum(outer_part, "tensor")
+    outer_rows = outer_part
+    for hop in (1, 2):
+        outer_rows = outer_rows + lax.ppermute(
+            outer_rows, "tensor", [(dev, dev ^ hop) for dev in range(4)]
+        )
     final, normal_two, inverse_two = layer_norm(
         normed + (outer_rows + outer_bias), second_gain, second_shift
     )

time: 1570 us -> 1840 us (1.17)
  waiting for transfers between devices: 1040 us -> 1290 us
    ppermute x0 -> x2, waiting for transfers between devices: none -> 529 us  [shards(): lax.ppermute(outer_rows, 'tensor', [(dev, dev ^ hop) for dev in range(4)])]
    psum x1 -> x0, waiting for transfers between devices: 280 us -> none  [shards(): outer_rows = lax.psum(outer_part, 'tensor')]
  transfers between devices with their start and end apart: 10 -> 11, of which waited for: 6 -> 7; matrix products, arithmetic and copies ran while one was open for 18% -> 16% of each run, Pallas kernels for 0% -> 0%
where the time goes in v1:
time: 1840 us; the launch traced here: 1830 us
  waiting for transfers between devices  1290 us (70%)
  matrix products  254 us (14%)
  other arithmetic  156 us (8%)
  local copies, waits for them, and re-layouts  55 us (3%)
  blocking collectives  49.4 us (3%)
    ppermute x2, waiting for transfers between devices, shards(): lax.ppermute(outer_rows, 'tensor', [(dev, dev ^ hop) for dev in range(4)])  529 us
    psum x1, waiting for transfers between devices, shards(): attention_whole = lax.psum(attention_part, 'tensor')  293 us
    psum x1, waiting for transfers between devices, shards(): normed_back = lax.psum(normed_part, 'tensor')  270 us
    psum x1, waiting for transfers between devices, shards(): lax.psum(input_part.astype(jnp.bfloat16), 'tensor').astype(jnp.float32)  156 us
    convert_element_type x4, other arithmetic, one_block(): score_grad = (probs * (prob_grad - centre)).astype(jnp.bfloat16)  42.8 us
    psum x1, blocking collectives, shards(): lax.psum((placed(jnp.sum(query_low.astype(jnp.float32), axis=0)), placed(...  40.3 us
    dot_general x4, matrix products, one_block(): jnp.einsum('qhd,khd->hqk', grad_block, values_split, preferred_element_ty...  39.8 us
  transfers between devices with their start and end apart: 11, of which 7 were waited for; matrix products, arithmetic and copies ran while one was open for 16% of the time, Pallas kernels for 0%

profile of v1, /device:TPU:0, one launch (start us, length us, event | category | flops | bytes accessed | tf_op | source)
XLA Modules:
  0.0 1829.2 jit_solution(17261489836693598658)
XLA Ops:
  25.2 55.2 %while.28 = (s32[]{:T(128)}, bf16[4,512,4,64]{1,3,2,0:T(8,128)(2,1)}, f32[4,4,512]{2,1,0:T(4,128)S(1)}, bf16[4,512,4,64]{1,3,2,0:T(8,128)(2,1)}, bf16[2048,4,64]...) while((s32[]{:T(128)}, bf16[4,512,4,64]{1,3,2,0:T(8,128)(2,1)}, ...), condition=%wide.region_3.4_spmd.clone, body=%wide.region_0.3_spmd.clone.sunk | while | flops 1124073472 | bytes 65872064 | solution.py:89
  33.2 4.9 fusion.138
  47.0 4.9 fusion.138
  60.8 4.9 fusion.138
  74.6 4.9 fusion.138
  83.9 5.6 fusion.70
  89.9 293.3 %all-reduce.5.cloned.1.call-done = f32[2048,1024]{1,0:T(8,128)} async-done(((f32[2048,1024]{1,0:T(8,128)}), f32[2048,1024]{1,0:T(8,128)}) %all-reduce.5.cloned.1.call-update) | async-done | bytes 8388624 | tf_op jit(solution)/shard_map/psum | solution.py:181
  383.2 5.9 fusion.54
  394.8 7.4 multiply_convert_fusion.1
  402.2 4.6 fusion.71
  410.0 179.0 %collective-permute-done = f32[2048,1024]{1,0:T(8,128)} collective-permute-done((f32[2048,1024]{1,0:T(8,128)S(1)}, f32[2048,1024]{1,0:T(8,128)}, u32[]{:S(2)}, u32[]{:S(2)}) %collective-permute-start) | collective-permute-done | bytes 8388640 | tf_op jit(solution)/shard_map/ppermute | solution.py:191
  589.0 12.0 add.205
  602.4 9.1 psum.100
  612.9 350.2 %collective-permute-done.1 = f32[2048,1024]{1,0:T(8,128)} collective-permute-done((f32[2048,1024]{1,0:T(8,128)}, f32[2048,1024]{1,0:T(8,128)}, u32[]{:S(2)}, u32[]{:S(2)}) %collective-permute-start.1) | collective-permute-done | bytes 8388640 | tf_op jit(solution)/shard_map/ppermute | solution.py:191
  963.2 9.2 fusion.69
  973.6 10.9 multiply_reduce_fusion.6
  990.6 11.3 convert_reduce_fusion
  1003.9 6.9 fusion.72
  1011.0 9.4 convolution_convert_fusion.2
  1020.5 10.5 convolution_convert_fusion.3
  1031.3 270.0 %all-reduce.7.cloned.1.call-done = f32[2048,1024]{1,0:T(8,128)} async-done(((f32[2048,1024]{1,0:T(8,128)}), f32[2048,1024]{1,0:T(8,128)}) %all-reduce.7.cloned.1.call-update) | async-done | bytes 8388624 | tf_op jit(solution)/shard_map/psum | solution.py:209
  1301.3 16.3 multiply_reduce_fusion.5
  1317.7 9.8 fusion.67
  1341.4 166.7 %while.29 = (s32[]{:T(128)}, f32[2048,4,64]{0,2,1:T(8,128)S(1)}, f32[2048,4,64]{0,2,1:T(8,128)}, bf16[4,512,4,64]{1,3,2,0:T(8,128)(2,1)}, bf16[4,512,4,64]{1,3,2...) while((s32[]{:T(128)}, f32[2048,4,64]{0,2,1:T(8,128)S(1)}, ...), condition=%wide.region_19.20_spmd.clone, body=%wide.region_17.19_spmd.clone.sunk | while | flops 2750021632 | bytes 180945136 | solution.py:129
  1346.3 5.8 fusion.150
  1352.1 10.1 multiply_reduce_fusion.8
  1362.2 11.0 multiply_convert_fusion.3
  1373.2 7.2 fusion.151
  1388.0 6.2 fusion.150
  1394.2 9.9 multiply_reduce_fusion.8
  1404.1 10.6 multiply_convert_fusion.3
  1414.7 7.1 fusion.151
  1429.4 6.2 fusion.150
  1435.6 9.9 multiply_reduce_fusion.8
  1445.5 10.6 multiply_convert_fusion.3
  1456.2 7.1 fusion.151
  1470.9 6.2 fusion.150
  1477.1 9.9 multiply_reduce_fusion.8
  1487.0 10.6 multiply_convert_fusion.3
  1497.6 7.1 fusion.151
  1527.9 5.7 fusion.74
  1538.1 4.5 fusion.73
  1542.7 9.1 add_convert_fusion
  1556.8 4.6 dynamic-slice_reduce_fusion
  1569.8 40.3 %all-reduce = (f32[]{:T(128)}, f32[1024]{0:T(1024)}, f32[1024]{0:T(1024)}, f32[1024]{0:T(1024)}, f32[1024]{0:T(1024)}, /*index=5*/f32[1024]{0:T(1024)}, f32[4096...) all-reduce(f32[]{:T(128)} %get-tuple-element.344, ...), channel_id=1, replica_groups=mesh['dp'=8,'tensor'=4] {'dp','tensor'}, use_global_device_ids=true, to_apply=%region_10.11 | all-reduce | flops 12289 | bytes 98312 | tf_op jit(solution)/shard_map/psum | solution.py:264
  1614.3 8.8 reduce-scatter.23.cloned.1.call-done
  1624.8 35.5 %reduce-scatter.13.cloned.1.call-done = bf16[128,256]{1,0:T(8,128)(2,1)} async-done(((bf16[1024,256]{1,0:T(8,128)(2,1)}), bf16[128,256]{1,0:T(8,128)(2,1)}) %reduce-scatter.13.cloned.1.call-update) | async-done | bytes 65552 | tf_op jit(solution)/shard_map/reduce_scatter | solution.py:247
  1661.8 155.9 %all-reduce.9.cloned.1.call-done = bf16[2048,1024]{1,0:T(8,128)(2,1)} async-done(((bf16[2048,1024]{1,0:T(8,128)(2,1)}), bf16[2048,1024]{1,0:T(8,128)(2,1)}) %all-reduce.9.cloned.1.call-update) | async-done | bytes 4194320 | tf_op jit(solution)/shard_map/psum | solution.py:226
  (245 shorter events, 169.1 us)
Async XLA Ops:
  7.2 387.6 %copy-start = (bf16[1024,1024]{1,0:T(8,128)(2,1)S(1)}, bf16[1024,1024]{1,0:T(8,128)(2,1)}, u32[]{:S(2)}) copy-start(bf16[1024,1024]{1,0:T(8,128)(2,1)} %param.34) | copy-start | bytes 6291460
  7.2 376.0 %all-reduce.5.cloned.1.call-start = ((), (), s32[]{:S(2)}) async-start(), calls=%async_computation.6 | async-start | bytes 16777216 | tf_op jit(solution)/shard_map/psum | solution.py:181
  29.4 3.8 copy-start.11
  29.4 3.8 copy-start.22
  43.2 3.8 copy-start.11
  43.2 3.8 copy-start.22
  57.0 3.8 copy-start.11
  57.0 3.8 copy-start.22
  70.8 3.8 copy-start.22
  83.8 6.0 copy-start.30
  83.8 6.0 copy-start.31
  83.8 6.0 copy-start.32
  83.8 6.1 copy-start.33
  89.5 1211.8 %all-reduce.7.cloned.1.call-start = ((), (), s32[]{:S(2)}) async-start(), calls=%async_computation.7 | async-start | bytes 16777216 | tf_op jit(solution)/shard_map/psum | solution.py:209
  383.2 7.0 copy-start.8
  383.2 8.2 copy-start.10
  394.7 12.0 copy-start.5
  394.8 7.4 copy-start.37
  402.1 4.6 copy-start.39
  406.8 206.0 %copy-start.34 = (bf16[1024]{0:T(1024)(128)(2,1)S(1)}, bf16[1024]{0:T(1024)(128)(2,1)}, u32[]{:S(2)}) copy-start(bf16[1024]{0:T(1024)(128)(2,1)} %param.38) | copy-start | bytes 6148
  406.8 206.0 %copy-start.35 = (bf16[1024]{0:T(1024)(128)(2,1)S(1)}, bf16[1024]{0:T(1024)(128)(2,1)}, u32[]{:S(2)}) copy-start(bf16[1024]{0:T(1024)(128)(2,1)} %param.37) | copy-start | bytes 6148
  406.8 206.0 %copy-start.36 = (bf16[1024]{0:T(1024)(128)(2,1)S(1)}, bf16[1024]{0:T(1024)(128)(2,1)}, u32[]{:S(2)}) copy-start(bf16[1024]{0:T(1024)(128)(2,1)} %param.39) | copy-start | bytes 6148
  406.8 182.2 %collective-permute-start = (f32[2048,1024]{1,0:T(8,128)S(1)}, f32[2048,1024]{1,0:T(8,128)}, u32[]{:S(2)}, u32[]{:S(2)}) collective-permute-start(f32[2048,1024]{1,0:T(8,128)S(1)} %fusion.71), channel_id=1, source_target_pairs={{0,1},{1,0},{2,3},{3,2},{4,5},{5,4},{6,7},{7,6},{8,9},{9,8},{10,11... | collective-permute-start | bytes 25165832 | tf_op jit(solution)/shard_map/ppermute | solution.py:191
  601.0 362.2 %collective-permute-start.1 = (f32[2048,1024]{1,0:T(8,128)}, f32[2048,1024]{1,0:T(8,128)}, u32[]{:S(2)}, u32[]{:S(2)}) collective-permute-start(f32[2048,1024]{1,0:T(8,128)} %add.205), channel_id=1, source_target_pairs={{0,2},{1,3},{2,0},{3,1},{4,6},{5,7},{6,4},{7,5},{8,10},{9,11},{10,... | collective-permute-start | bytes 25165832 | tf_op jit(solution)/shard_map/ppermute | solution.py:191
  612.9 360.7 %copy-start.28 = (pred[2048]{0:T(1024)(128)(4,1)}, pred[2048]{0:T(1024)(128)(4,1)S(1)}, u32[]{:S(2)}) copy-start(pred[2048]{0:T(1024)(128)(4,1)S(1)} %iota_compare_fusion.2) | copy-start | bytes 6148
  984.5 6.1 copy-start.7
  984.5 6.1 copy-start.38
  990.6 11.4 copy-start.14
  1010.8 550.6 %reduce-scatter.17.cloned.1.call-start = ((), (), s32[]{:S(2)}) async-start(), calls=%async_computation.11 | async-start | bytes 2359296 | tf_op jit(solution)/shard_map/reduce_scatter | solution.py:253
  1020.5 542.7 %reduce-scatter.15.cloned.1.call-start = ((), (), s32[]{:S(2)}) async-start(), calls=%async_computation.10 | async-start | bytes 2359296 | tf_op jit(solution)/shard_map/reduce_scatter | solution.py:250
  1031.0 579.8 %reduce-scatter.19.cloned.1.call-start = ((), (), s32[]{:S(2)}) async-start(), calls=%async_computation.12 | async-start | bytes 589824
  1317.7 11.8 copy-start.24
  1373.2 7.2 copy-start.2
  1414.7 7.1 copy-start.2
  1456.2 7.2 copy-start.2
  1497.6 7.2 copy-start.2
  1515.9 96.7 %reduce-scatter.21.cloned.1.call-start = ((), (), s32[]{:S(2)}) async-start(), calls=%async_computation.13 | async-start | bytes 589824
  1522.4 100.7 %reduce-scatter.23.cloned.1.call-start = ((), (), s32[]{:S(2)}) async-start(), calls=%async_computation.14 | async-start | bytes 589824
  1526.8 6.8 copy-start.17
  1527.9 10.2 copy-start.19
  1533.5 4.6 copy-start.25
  1533.6 126.8 %reduce-scatter.13.cloned.1.call-start = ((), (), s32[]{:S(2)}) async-start(), calls=%async_computation.9 | async-start | bytes 589824 | tf_op jit(solution)/shard_map/reduce_scatter | solution.py:247
  1538.1 4.6 copy-start.21
  1538.1 4.6 copy-start.27
  1542.6 10.1 copy-start.29
  1542.7 275.1 %all-reduce.9.cloned.1.call-start = ((), (), s32[]{:S(2)}) async-start(), calls=%async_computation.8 | async-start | bytes 8388608 | tf_op jit(solution)/shard_map/psum | solution.py:226
  1551.8 13.2 copy-start.12
  1556.8 264.5 %copy-start.1 = (bf16[1024,1024]{1,0:T(8,128)(2,1)S(1)}, bf16[1024,1024]{1,0:T(8,128)(2,1)}, u32[]{:S(2)}) copy-start(bf16[1024,1024]{1,0:T(8,128)(2,1)} %param.34) | copy-start | bytes 6291460
  (22 other events, 44.3 us)
Sparse Core Ops, SparseCore 0:
  89.6 293.5 all-reduce.4
  1010.9 290.3 all-reduce.6
  1304.6 40.0 reduce-scatter.16
  1347.9 41.1 reduce-scatter.14
  1516.0 32.6 reduce-scatter.18
  1551.6 34.2 reduce-scatter.20
  1588.9 34.1 reduce-scatter.22
  1626.2 34.1 reduce-scatter.12
  1662.7 154.9 all-reduce.8
